TPU v7x, 128 devices: a whole 4x4x4 slice. The times are simulated.
128 devices in a mesh: width: 8 (over y, x_lo), store: 16 (over x_hi, z, core).
Axes of the slice: x: 4 (x_hi: 2, x_lo: 2; x = x_hi * 2 + x_lo), y: 4, z: 4, core: 2. Of those that a mesh axis runs over, the one named last changes fastest.
Arguments:
- activations: bfloat16 [128, 512, 8192], P('store', None, 'width'), may hold values from -6 to 6
- out_grads: bfloat16 [128, 512, 8192], P('store', None, 'width'), may hold values from -6 to 6
- proj_in: bfloat16 [8192, 64], P('width'), may hold values from -0.0625 to 0.0625
- proj_out: bfloat16 [8192, 64], P('width'), may hold values from -0.0625 to 0.0625
- fisher_inv: float32 [4096, 4096], P('store', 'width'), may hold values from -0.09375 to 0.09375
- grad_store: float32 [32768, 4096], P('store', 'width'), may hold values from -6 to 6
Outputs:
- scores: float32 [128, 32768], P('width', 'store')
All inputs are finite; a program needn't handle non-finite values.
Results may differ from a plain program's by a relative error of at most 0.0003.
Values sent between devices are 32-bit elements; how exact they have to be, the bound alone decides.
No kernel may reach another device: no remote copies, remote signals or barrier semaphores. Data moves between devices by JAX's collectives and lax.ppermute only.
A program may use at most 128 MiB of HBM per device.

v0:
```python
import jax
import jax.numpy as jnp
from jax import lax
from jax.sharding import PartitionSpec as P

RANK = 64
SEQ = 512
COORD = 4096


def outer_mean(paired):
    grad_side = paired[:, :, :RANK]
    act_side = paired[:, :, RANK:]
    result = jnp.einsum("qti,qtj->qij", grad_side, act_side, precision=lax.Precision.HIGHEST) / SEQ
    return result.reshape(paired.shape[0], COORD)


def body(activations, out_grads, proj_in, proj_out, fisher_inv, grad_store):
    act_proj = jnp.einsum("qtd,dr->qtr", activations, proj_in, preferred_element_type=jnp.float32)
    grad_proj = jnp.einsum("qtd,dr->qtr", out_grads, proj_out, preferred_element_type=jnp.float32)
    paired = jnp.concatenate([grad_proj, act_proj], axis=2)
    summed = lax.psum(paired, "width")
    gradient = outer_mean(summed)
    own_rows = jnp.dot(
        gradient,
        lax.all_gather(fisher_inv, "store", axis=0, tiled=True),
        precision=lax.Precision.HIGHEST,
    )
    precond = lax.all_gather(own_rows, "store", axis=0, tiled=True)
    return lax.psum_scatter(
        jnp.dot(precond, grad_store.T, precision=lax.Precision.HIGHEST),
        "width",
        scatter_dimension=0,
        tiled=True,
    )


def solution(mesh):
    placed = (
        P("store", None, "width"),
        P("store", None, "width"),
        P("width", None),
        P("width", None),
        P("store", "width"),
        P("store", "width"),
    )
    return jax.shard_map(
        body, mesh=mesh, in_specs=placed, out_specs=P("width", "store"), check_vma=False
    )
```

profile of v0, /device:TPU:0, one launch (start us, length us, event | category | flops | bytes accessed | tf_op | source)
XLA Modules:
  0.0 237.1 jit_solution(8299051570266374264)
XLA Ops:
  7.4 0.0 copy-start
  7.4 0.0 copy-start.3
  7.4 0.0 all-reduce.2.cloned.1.call-start
  7.4 0.9 copy-done
  8.3 6.2 %fusion.2 = f32[8,512,64]{1,2,0:T(8,128)S(1)} fusion(bf16[8,512,1024]{2,1,0:T(8,128)(2,1)} %param.6, bf16[1024,64]{0,1:T(8,128)(2,1)S(1)} %copy-done), kind=kOutput, calls=%fused_computation.4 | convolution fusion | flops 536870912 | bytes 9568256 | tf_op jit(solution)/shard_map/qtd,dr->qtr/dot_general | solution.py:19
  14.5 0.0 copy-done.3
  14.5 0.0 copy-done.1
  14.5 2.7 %fusion.4 = f32[8,512,64]{1,2,0:T(8,128)S(1)} fusion(bf16[8,512,1024]{2,1,0:T(8,128)(2,1)S(1)} %copy-done.1, bf16[1024,64]{0,1:T(8,128)(2,1)S(1)} %copy-done.3), kind=kOutput, calls=%fused_computation.6 | convolution fusion | flops 536870912 | bytes 9568256 | tf_op jit(solution)/shard_map/qtd,dr->qtr/dot_general | solution.py:20
  17.1 1.5 pad_maximum_fusion
  18.6 0.0 all-reduce.2.cloned.1.call-update
  18.7 0.0 all-gather.2.cloned.1.call-start
  18.7 0.5 all-gather.2.cloned.1.call-update
  19.2 0.0 reduce-scatter.2.cloned.1.call-start
  19.3 134.7 %all-reduce.2.cloned.1.call-done = f32[8,512,128]{1,2,0:T(8,128)} async-done(((f32[8,512,128]{1,2,0:T(8,128)}), f32[8,512,128]{1,2,0:T(8,128)}) %all-reduce.2.cloned.1.call-update) | async-done | bytes 2097168 | tf_op jit(solution)/shard_map/psum | solution.py:22
  154.0 2.6 %convolution_multiply_fusion = f32[8,64,64]{2,1,0:T(8,128)S(1)} fusion(f32[8,512,128]{1,2,0:T(8,128)} %all-reduce.2.cloned.1.call-done), kind=kOutput, calls=%fused_computation.1 | convolution fusion | flops 201359360 | bytes 2228224 | tf_op jit(solution)/shard_map/qti,qtj->qij/dot_general | solution.py:14
  156.7 0.1 reshape.3
  156.8 0.0 all-gather.2.cloned.1.call-done
  156.8 0.0 copy-start.2
  156.8 5.8 %fusion.6 = f32[8,512]{1,0:T(8,128)S(1)} fusion(f32[8,4096]{1,0:T(8,128)S(1)} %reshape.3, f32[4096,512]{1,0:T(8,128)} %all-gather.2.cloned.1.call-done), kind=kOutput, calls=%fused_computation.8 | convolution fusion | flops 201326592 | bytes 8536064 | tf_op jit(solution)/shard_map/dot_general | solution.py:24
  162.7 24.7 %all_gather.7 = f32[128,512]{1,0:T(8,128)S(1)} all-gather(f32[8,512]{1,0:T(8,128)S(1)} %fusion.6), channel_id=1, replica_groups=mesh['width'=8,'store'=16] {'store'}, dimensions={0}, use_global_device_ids=true | all-gather | bytes 278528 | tf_op jit(solution)/shard_map/all_gather | solution.py:29
  187.4 0.0 copy-done.2
  187.4 5.3 %fusion.7 = f32[128,2048]{1,0:T(8,128)} fusion(f32[128,512]{1,0:T(8,128)S(1)} %all_gather.7, f32[2048,512]{1,0:T(8,128)S(1)} %copy-done.2), kind=kOutput, calls=%fused_computation.9 | convolution fusion | flops 1610612736 | bytes 5505024 | tf_op jit(solution)/shard_map/dot_general | solution.py:31
  192.7 0.0 reduce-scatter.2.cloned.1.call-update
  192.7 36.9 %reduce-scatter.2.cloned.1.call-done = f32[16,2048]{1,0:T(8,128)} async-done(((f32[128,2048]{1,0:T(8,128)}), f32[16,2048]{1,0:T(8,128)}) %reduce-scatter.2.cloned.1.call-update) | async-done | bytes 131088 | tf_op jit(solution)/shard_map/reduce_scatter | solution.py:30
  (1 shorter events, 0.0 us)
Async XLA Ops:
  7.4 0.9 copy-start
  7.4 7.1 %copy-start.3 = (bf16[1024,64]{0,1:T(8,128)(2,1)S(1)}, bf16[1024,64]{0,1:T(8,128)(2,1)}, u32[]{:S(2)}) copy-start(bf16[1024,64]{0,1:T(8,128)(2,1)} %param.9) | copy-start | bytes 393220
  7.4 146.7 %all-reduce.2.cloned.1.call-start = ((), (), s32[]{:S(2)}) async-start(), calls=%async_computation.1 | async-start | bytes 4194304 | tf_op jit(solution)/shard_map/psum | solution.py:22
  8.3 6.2 %copy-start.1 = (bf16[8,512,1024]{2,1,0:T(8,128)(2,1)S(1)}, bf16[8,512,1024]{2,1,0:T(8,128)(2,1)}, u32[]{:S(2)}) copy-start(bf16[8,512,1024]{2,1,0:T(8,128)(2,1)} %param.7) | copy-start | bytes 25165828
  18.7 138.1 %all-gather.2.cloned.1.call-start = ((), (), s32[]{:S(2)}) async-start(), calls=%async_computation.2 | async-start | bytes 8912896 | tf_op jit(solution)/shard_map/all_gather | solution.py:26
  19.2 210.4 %reduce-scatter.2.cloned.1.call-start = ((), (), s32[]{:S(2)}) async-start(), calls=%async_computation.3 | async-start | bytes 1179648 | tf_op jit(solution)/shard_map/reduce_scatter | solution.py:30
  156.8 30.6 %copy-start.2 = (f32[2048,512]{1,0:T(8,128)S(1)}, f32[2048,512]{1,0:T(8,128)}, u32[]{:S(2)}) copy-start(f32[2048,512]{1,0:T(8,128)} %param.11) | copy-start | bytes 12582916
Sparse Core Ops, SparseCore 0:
  18.8 135.2 all-reduce.1
  192.8 36.7 reduce-scatter.1
Sparse Core Ops, SparseCore 1:
  21.6 80.3 all-gather.1
where the time goes:
time: 237 us
  waiting for transfers between devices  172 us (73%)
  blocking collectives  24.7 us (10%)
  matrix products  22.6 us (10%)
  between operations  14.9 us (6%)
    psum x1, waiting for transfers between devices, body(): summed = lax.psum(paired, 'width')  135 us
    reduce_scatter x1, waiting for transfers between devices, body(): lax.psum_scatter(jnp.dot(precond, grad_store.T, precision=lax.Precision.H...  36.9 us
    all_gather x1, blocking collectives, body(): precond = lax.all_gather(own_rows, 'store', axis=0, tiled=True)  24.7 us
    dot_general x1, matrix products, body(): jnp.einsum('qtd,dr->qtr', activations, proj_in, preferred_element_type=jn...  6.19 us
    dot_general x1, matrix products, body(): jnp.dot(gradient, lax.all_gather(fisher_inv, 'store', axis=0, tiled=True)...  5.84 us
    dot_general x1, matrix products, body(): jnp.dot(precond, grad_store.T, precision=lax.Precision.HIGHEST)  5.31 us
  transfers between devices with their start and end apart: 3, of which 2 were waited for; matrix products, arithmetic and copies ran while one was open for 1% of the time, Pallas kernels for 0%

commit v1 on v0

v1 whole, which is shorter than its diff:
```python
import functools

import jax
import jax.numpy as jnp
from jax import lax
from jax.experimental import pallas as pl
from jax.experimental.pallas import tpu as pltpu
from jax.sharding import PartitionSpec as P

RANK = 64
SEQ = 512
WIDTH = 8
STORE = 16
NEAR = 8
MIB = 1024 * 1024


NT = (((1,), (1,)), ((), ()))
NN = (((1,), (0,)), ((), ()))


def split(x):
    high = x.astype(jnp.bfloat16)
    low = (x - high.astype(jnp.float32)).astype(jnp.bfloat16)
    return high, low


def dot(a, b, dims):
    return lax.dot_general(a, b, dims, preferred_element_type=jnp.float32)


def dot3(a, b, dims):
    a_high, a_low = split(a)
    b_high, b_low = split(b)
    return dot(a_high, b_high, dims) + (dot(a_high, b_low, dims) + dot(a_low, b_high, dims))


def limit(mib):
    return pltpu.CompilerParams(vmem_limit_bytes=mib * MIB)


def hbm(x):
    return pltpu.with_memory_space_constraint(x, pltpu.HBM)


VMEM = pl.BlockSpec(memory_space=pltpu.VMEM)
SMEM = pl.BlockSpec(memory_space=pltpu.SMEM)
HBM = pl.BlockSpec(memory_space=pltpu.HBM)


def project_first_kernel(k, place_ref, act_ref, grad_ref, in_ref, out_ref, *refs):
    result_ref, tokens, weights, token_sem, weight_sem = refs
    weight_copies = [
        pltpu.make_async_copy(source, weights.at[side], weight_sem.at[side])
        for side, source in enumerate((out_ref, in_ref))
    ]
    copies = [
        pltpu.make_async_copy(source.at[place_ref[0] ^ k], tokens.at[side], token_sem.at[side])
        for side, source in enumerate((grad_ref, act_ref))
    ]
    for copy in weight_copies + copies:
        copy.start()
    for side in range(2):
        weight_copies[side].wait()
        copies[side].wait()
        result_ref[side * RANK : (side + 1) * RANK, :] = dot(weights[side], tokens[side], NT)


def project_first(k, place, activations, out_grads, proj_in_t, proj_out_t):
    depth = activations.shape[2]
    return pl.pallas_call(
        functools.partial(project_first_kernel, k),
        out_shape=jax.ShapeDtypeStruct((2 * RANK, SEQ), jnp.float32),
        in_specs=[SMEM, HBM, HBM, HBM, HBM],
        out_specs=VMEM,
        scratch_shapes=[
            pltpu.VMEM((2, SEQ, depth), jnp.bfloat16),
            pltpu.VMEM((2, RANK, depth), jnp.bfloat16),
            pltpu.SemaphoreType.DMA((2,)),
            pltpu.SemaphoreType.DMA((2,)),
        ],
        compiler_params=limit(6),
        cost_estimate=project_cost(1, depth),
        name="project_first",
    )(place, hbm(activations), hbm(out_grads), hbm(proj_in_t), hbm(proj_out_t))


def project_cost(count, depth):
    return pl.CostEstimate(
        flops=4 * count * SEQ * depth * RANK,
        bytes_accessed=4 * count * SEQ * depth,
        transcendentals=0,
    )


def project_kernel(group, place_ref, act_ref, grad_ref, in_ref, out_ref, *result_refs):
    for k, result_ref in zip(group, result_refs, strict=True):
        query = place_ref[0] ^ k
        result_ref[:RANK, :] = dot(out_ref[...], grad_ref[query], NT)
        result_ref[RANK:, :] = dot(in_ref[...], act_ref[query], NT)


def project(group, place, activations, out_grads, proj_in_t, proj_out_t):
    count = len(group)
    part = jax.ShapeDtypeStruct((2 * RANK, SEQ), jnp.float32)
    return pl.pallas_call(
        functools.partial(project_kernel, group),
        out_shape=(part,) * count,
        in_specs=[SMEM, VMEM, VMEM, VMEM, VMEM],
        out_specs=(VMEM,) * count,
        compiler_params=limit(20),
        cost_estimate=project_cost(count, activations.shape[2]),
        name="project",
    )(place, activations, out_grads, proj_in_t, proj_out_t)


def gradient_kernel(place_ref, *refs):
    *parts, result_ref, held = refs
    total = parts[0][...]
    for part in parts[1:]:
        total = total + part[...]
    held[...] = dot3(total[:RANK], total[RANK:], NT) * (1.0 / SEQ)
    half = RANK // 2
    pairs = jnp.concatenate(
        [held[pl.ds(0, half, stride=2), :], held[pl.ds(1, half, stride=2), :]], axis=1
    )
    row = lax.broadcasted_iota(jnp.int32, pairs.shape, 0)
    for bit in (1, 2, 4):
        far = 2 * bit
        swapped = jnp.where(
            (row & far) == 0, pltpu.roll(pairs, half - far, 0), pltpu.roll(pairs, far, 0)
        )
        pairs = jnp.where((place_ref[1] & bit) != 0, swapped, pairs)
    for side in range(2):
        block = pairs[side * 16 : (side + 1) * 16, :]
        for i in range(WIDTH):
            result_ref[side * WIDTH + i] = block


def gradient(place, parts):
    return pl.pallas_call(
        gradient_kernel,
        out_shape=jax.ShapeDtypeStruct((2 * WIDTH, 16, 128), jnp.float32),
        in_specs=[SMEM] + [VMEM] * len(parts),
        out_specs=VMEM,
        scratch_shapes=[pltpu.VMEM((RANK, RANK), jnp.float32)],
        compiler_params=limit(4),
        name="gradient",
    )(place, *parts)


def partial_kernel(rows_ref, *refs):
    *fisher_refs, result_ref = refs
    high, low = split(rows_ref[...])
    total = None
    for i, fisher_ref in enumerate(fisher_refs):
        f_high, f_low = split(fisher_ref[...])
        for side in range(2):
            rows = 2 * i + side
            span = slice(side * 128, (side + 1) * 128)
            a_high, a_low = high[:, rows, :], low[:, rows, :]
            term = dot(a_high, f_high[span], NN) + (
                dot(a_high, f_low[span], NN) + dot(a_low, f_high[span], NN)
            )
            total = term if total is None else total + term
    for i in range(STORE):
        result_ref[i] = total


def partial_precond(rows, fisher):
    columns = fisher[0].shape[1]
    return pl.pallas_call(
        partial_kernel,
        out_shape=jax.ShapeDtypeStruct((STORE, 2 * WIDTH, columns), jnp.float32),
        in_specs=[VMEM] * (1 + len(fisher)),
        out_specs=VMEM,
        compiler_params=limit(10),
        name="partial_precond",
    )(rows, *fisher)


def score_kernel(place_ref, halves_ref, store_ref, *refs):
    *result_refs, p_high, p_low = refs
    rows = 8
    for k in range(WIDTH):
        owner = place_ref[0] ^ k
        offset = pl.ds(pl.multiple_of((owner >> 2) * rows, rows), rows)
        for core in range(2):
            near = ((2 * owner) & (NEAR - 1)) + core
            block = halves_ref[near, offset, :] + halves_ref[NEAR + near, offset, :]
            span = slice((2 * k + core) * rows, (2 * k + core + 1) * rows)
            p_high[span, :] = block.astype(jnp.bfloat16).astype(jnp.float32)
            p_low[span, :] = block - p_high[span, :]
    a_high = p_high[...].astype(jnp.bfloat16)
    a_low = p_low[...].astype(jnp.bfloat16)
    width = 512
    for n in range(store_ref.shape[0] // width):
        span = slice(n * width, (n + 1) * width)
        b_high, b_low = split(store_ref[span, :])
        total = dot(a_high, b_high, NT) + (dot(a_high, b_low, NT) + dot(a_low, b_high, NT))
        for k in range(WIDTH):
            result_refs[k][:, span] = total[16 * k : 16 * (k + 1), :]


def scores(place, halves, store):
    examples, columns = store.shape
    block = jax.ShapeDtypeStruct((16, examples), jnp.float32)
    return pl.pallas_call(
        score_kernel,
        out_shape=(block,) * WIDTH,
        in_specs=[SMEM, VMEM, VMEM],
        out_specs=(VMEM,) * WIDTH,
        scratch_shapes=[pltpu.VMEM((128, columns), jnp.float32)] * 2,
        compiler_params=limit(12),
        name="scores",
    )(place, halves, store)


def exchange(x, axis, k, size):
    return lax.ppermute(x, axis, [(i, i ^ k) for i in range(size)])


ORDER = (5, 3, 7, 1, 4, 6, 2)
GROUPS = (((5,), 4), ((3,), 2), ((7, 1), 6), ((4, 6), 0), ((2,), 0), ((0,), 0))


def body(activations, out_grads, proj_in, proj_out, fisher_inv, grad_store):
    place = jnp.stack([lax.axis_index("width"), lax.axis_index("store") & (NEAR - 1)])
    proj_in_t, proj_out_t = proj_in.T, proj_out.T
    weights = (activations, out_grads, proj_in_t, proj_out_t)
    parts, fisher = {}, {0: fisher_inv}
    for n, (group, far) in enumerate(GROUPS):
        if n:
            projected = project(group, place, *weights)
        else:
            projected = (project_first(group[0], place, *weights),)
        for k, part in zip(group, projected, strict=True):
            parts[k] = exchange(part, "width", k, WIDTH) if k else part
        if far:
            fisher[far] = exchange(fisher_inv, "store", far, STORE)
    last, *blocks = lax.optimization_barrier((parts[0], *(fisher[k] for k in (0, 2, 4, 6))))
    for k, block in zip((0, 2, 4, 6), blocks, strict=True):
        fisher[k + 1] = exchange(block, "store", 1, STORE)
    outgoing = gradient(place, [parts[k] for k in range(WIDTH)])
    groups = [
        [(side * NEAR + i) * WIDTH + w for side in range(2) for w in range(WIDTH)]
        for i in range(NEAR)
    ]
    rows = lax.all_to_all(outgoing, ("store", "width"), 0, 0, axis_index_groups=groups)
    halves = partial_precond(rows, [fisher[i] for i in range(NEAR)])
    halves = lax.all_to_all(halves, "store", 0, 0)
    blocks = scores(place, halves, grad_store)
    total = blocks[0]
    for block in [exchange(blocks[k], "width", k, WIDTH) for k in ORDER]:
        total = total + block
    return total


def solution(mesh):
    placed = (
        P("store", None, "width"),
        P("store", None, "width"),
        P("width", None),
        P("width", None),
        P("store", "width"),
        P("store", "width"),
    )
    return jax.shard_map(
        body, mesh=mesh, in_specs=placed, out_specs=P("width", "store"), check_vma=False
    )
```

time: 237 us -> 114 us (0.48)
  waiting for transfers between devices: 172 us -> 25.2 us
  starting transfers between devices: 0.09 us -> 30.8 us
  matrix products: 22.6 us -> 0 us
  Pallas kernels: 0 us -> 16 us
  between operations: 14.9 us -> 0.19 us
  local copies, waits for them, and re-layouts: 1.03 us -> 8.61 us
  blocking collectives: 24.7 us -> 31.5 us
    psum x1 -> x0, waiting for transfers between devices: 135 us -> none  [body(): summed = lax.psum(paired, 'width')]
    reduce_scatter x1 -> x0, waiting for transfers between devices: 36.9 us -> none  [body(): lax.psum_scatter(jnp.dot(precond, grad_store.T, precision=lax.Precision.H...]
    all_to_all x0 -> x2, blocking collectives: none -> 31.5 us  [the longest x1 16.9 us: body(): halves = lax.all_to_all(halves, 'store', 0, 0)]
    ppermute x0 -> x21, starting transfers between devices: none -> 30.8 us  [exchange(): return lax.ppermute(x, axis, [(i, i ^ k) for i in range(size)])]
    ppermute x0 -> x21, waiting for transfers between devices: none -> 25.2 us  [exchange(): return lax.ppermute(x, axis, [(i, i ^ k) for i in range(size)])]
    all_gather x1 -> x0, blocking collectives: 24.7 us -> none  [body(): precond = lax.all_gather(own_rows, 'store', axis=0, tiled=True)]
    dot_general x5 -> x0, matrix products: 22.6 us -> none  [the longest x1 6.19 us: body(): jnp.einsum('qtd,dr->qtr', activations, proj_in, preferred_element_type=jn...]
    pallas_call x0 -> x9, Pallas kernels: none -> 16 us  [the longest x5 7.76 us: project(): pl.pallas_call(functools.partial(project_kernel, group), out_shape=(part,...]
  transfers between devices with their start and end apart: 3 -> 21, of which waited for: 2 -> 9; matrix products, arithmetic and copies ran while one was open for 1% -> 0% of each run, Pallas kernels for 0% -> 11%
where the time goes in v1:
time: 114 us; the launch traced here: 113 us
  blocking collectives  31.5 us (28%)
  starting transfers between devices  30.8 us (27%)
  waiting for transfers between devices  25.2 us (22%)
  Pallas kernels  16 us (14%)
  local copies, waits for them, and re-layouts  8.61 us (8%)
    ppermute x21, starting transfers between devices, exchange(): return lax.ppermute(x, axis, [(i, i ^ k) for i in range(size)])  30.8 us
    ppermute x21, waiting for transfers between devices, exchange(): return lax.ppermute(x, axis, [(i, i ^ k) for i in range(size)])  25.2 us
    all_to_all x1, blocking collectives, body(): halves = lax.all_to_all(halves, 'store', 0, 0)  16.9 us
    all_to_all x1, blocking collectives, body(): lax.all_to_all(outgoing, ('store', 'width'), 0, 0, axis_index_groups=groups)  14.6 us
    unnamed x24, local copies, waits for them, and re-layouts  8.61 us
    pallas_call x5, Pallas kernels, project(): pl.pallas_call(functools.partial(project_kernel, group), out_shape=(part,...  7.76 us
    pallas_call x1, Pallas kernels, project_first(): pl.pallas_call(functools.partial(project_first_kernel, k), out_shape=jax....  3.5 us
    pallas_call x1, Pallas kernels, scores(): pl.pallas_call(score_kernel, out_shape=(block,) * WIDTH, in_specs=[SMEM,...  2.77 us
  transfers between devices with their start and end apart: 21, of which 9 were waited for; matrix products, arithmetic and copies ran while one was open for 0% of the time, Pallas kernels for 11%

profile of v1, /device:TPU:0, one launch (start us, length us, event | category | flops | bytes accessed | tf_op | source)
XLA Modules:
  0.0 113.0 jit_solution(4761819782897693127)
XLA Ops:
  0.0 4.1 %collective-permute-start.9 = (f32[256,512]{1,0:T(8,128)}, f32[256,512]{1,0:T(8,128)S(1)}, u32[]{:S(2)}, u32[]{:S(2)}) collective-permute-start(f32[256,512]{1,0:T(8,128)} %refs_0_.1), channel_id=1, source_target_pairs={{0,6},{1,7},{2,4},{3,5},{4,2},{5,3},{6,0},{7,1},{8,14},{9,15},{10,... | collective-permute-start | bytes 1572872 | tf_op jit(solution)/shard_map/ppermute | solution.py:220
  5.1 3.4 %copy-done = bf16[8,512,1024]{2,1,0:T(8,128)(2,1)S(1)} copy-done((bf16[8,512,1024]{2,1,0:T(8,128)(2,1)S(1)}, bf16[8,512,1024]{2,1,0:T(8,128)(2,1)}, u32[]{:S(2)}) %copy-start) | copy-done | bytes 8388632
  8.5 3.4 %copy-done.1 = bf16[8,512,1024]{2,1,0:T(8,128)(2,1)S(1)} copy-done((bf16[8,512,1024]{2,1,0:T(8,128)(2,1)S(1)}, bf16[8,512,1024]{2,1,0:T(8,128)(2,1)}, u32[]{:S(2)}) %copy-start.1) | copy-done | bytes 8388632
  15.0 1.7 %collective-permute-start.1 = (f32[128,512]{1,0:T(8,128)S(1)}, f32[128,512]{1,0:T(8,128)S(1)}, u32[]{:S(2)}, u32[]{:S(2)}) collective-permute-start(f32[128,512]{1,0:T(8,128)S(1)} %project.7), channel_id=1, source_target_pairs={{0,32},{16,48},{32,0},{48,16},{64,96},{80,112},{96,64},{112,80},{1... | collective-permute-start | bytes 786440 | tf_op jit(solution)/shard_map/ppermute | solution.py:220
  16.6 1.3 %project.8 = f32[128,512]{1,0:T(8,128)S(1)} custom-call(s32[2]{0:T(128)S(1)} %pad_add_fusion.place_ref, bf16[8,512,1024]{2,1,0:T(8,128)(2,1)S(1)} %copy-done, bf16[8,512,1024]{2,1,0:T(8,128)(2,1)S(1)} %copy-done.1, bf16[64,1024]{1,0:T(8,128)(2,1)S(1)} %bitcast.10, bf16[64,1024]{1,0:T(8,128)(2,1)S(1)} %bitcast.16), custom_call_target="tpu_custom_call" | custom-call | flops 134217728 | bytes 2097152 | tf_op jit(solution)/shard_map/project/pallas_call | solution.py:106
  17.9 1.5 %collective-permute-start.2 = (f32[128,512]{1,0:T(8,128)S(1)}, f32[128,512]{1,0:T(8,128)S(1)}, u32[]{:S(2)}, u32[]{:S(2)}) collective-permute-start(f32[128,512]{1,0:T(8,128)S(1)} %project.8), channel_id=1, source_target_pairs={{0,48},{16,32},{32,16},{48,0},{64,112},{80,96},{96,80},{112,64},{1... | collective-permute-start | bytes 786440 | tf_op jit(solution)/shard_map/ppermute | solution.py:220
  19.4 1.9 %project.9 = (f32[128,512]{1,0:T(8,128)S(1)}, f32[128,512]{1,0:T(8,128)S(1)}) custom-call(s32[2]{0:T(128)S(1)} %pad_add_fusion.place_ref, bf16[8,512,1024]{2,1,0:T(8,128)(2,1)S(1)} %copy-done, bf16[8,512,1024]{2,1,0:T(8,128)(2,1)S(1)} %copy-done.1, bf16[64,1024]{1,0:T(8,128)(2,1)S(1)} %bitcast.11, bf16[64,1024]{1,0:T(8,128)(2,1)S(1)} %bitcast.17), custom_call_target="tpu_custom_call" | custom-call | flops 268435456 | bytes 4194304 | tf_op jit(solution)/shard_map/project/pallas_call | solution.py:106
  21.3 3.5 %project_first.1 = f32[128,512]{1,0:T(8,128)S(1)} custom-call(s32[2]{0:T(128)S(1)} %pad_add_fusion.place_ref, bf16[8,512,1024]{2,1,0:T(8,128)(2,1)} %act_ref.11, bf16[8,512,1024]{2,1,0:T(8,128)(2,1)} %grad_ref.11, bf16[64,1024]{1,0:T(8,128)(2,1)} %bitcast.8, bf16[64,1024]{1,0:T(8,128)(2,1)} %bitcast.14), custom_call_target="tpu_custom_call" | custom-call | flops 134217728 | bytes 2097152 | tf_op jit(solution)/shard_map/project_first/pallas_call | solution.py:71
  24.9 3.3 %collective-permute-done.1.refs_2_ = f32[128,512]{1,0:T(8,128)S(1)} collective-permute-done((f32[128,512]{1,0:T(8,128)S(1)}, f32[128,512]{1,0:T(8,128)S(1)}, u32[]{:S(2)}, u32[]{:S(2)}) %collective-permute-start.1) | collective-permute-done | bytes 262176 | tf_op jit(solution)/shard_map/ppermute | solution.py:220
  28.1 4.1 %collective-permute-start.4 = (f32[128,512]{1,0:T(8,128)S(1)}, f32[128,512]{1,0:T(8,128)S(1)}, u32[]{:S(2)}, u32[]{:S(2)}) collective-permute-start(f32[128,512]{1,0:T(8,128)S(1)} %project_first.1), channel_id=1, source_target_pairs={{0,80},{16,64},{32,112},{48,96},{64,16},{80,0},{96,48},{112,32},{1... | collective-permute-start | bytes 786440 | tf_op jit(solution)/shard_map/ppermute | solution.py:220
  32.6 3.0 %collective-permute-start.5 = (f32[128,512]{1,0:T(8,128)S(1)}, f32[128,512]{1,0:T(8,128)S(1)}, u32[]{:S(2)}, u32[]{:S(2)}) collective-permute-start(f32[128,512]{1,0:T(8,128)S(1)} %get-tuple-element.23), channel_id=1, source_target_pairs={{0,96},{16,112},{32,64},{48,80},{64,32},{80,48},{96,0},{112,16},{1... | collective-permute-start | bytes 786440 | tf_op jit(solution)/shard_map/ppermute | solution.py:220
  35.7 1.9 %project.6 = (f32[128,512]{1,0:T(8,128)S(1)}, f32[128,512]{1,0:T(8,128)S(1)}) custom-call(s32[2]{0:T(128)S(1)} %pad_add_fusion.place_ref, bf16[8,512,1024]{2,1,0:T(8,128)(2,1)S(1)} %bitcast.5, bf16[8,512,1024]{2,1,0:T(8,128)(2,1)S(1)} %bitcast.7, bf16[64,1024]{1,0:T(8,128)(2,1)S(1)} %bitcast.12, bf16[64,1024]{1,0:T(8,128)(2,1)S(1)} %bitcast.18), custom_call_target="tpu_custom_call" | custom-call | flops 268435456 | bytes 4194304 | tf_op jit(solution)/shard_map/project/pallas_call | solution.py:106
  38.2 1.3 %project.5.refs_0_ = f32[128,512]{1,0:T(8,128)S(1)} custom-call(s32[2]{0:T(128)S(1)} %pad_add_fusion.place_ref, bf16[8,512,1024]{2,1,0:T(8,128)(2,1)S(1)} %bitcast.5, bf16[8,512,1024]{2,1,0:T(8,128)(2,1)S(1)} %bitcast.7, bf16[64,1024]{1,0:T(8,128)(2,1)S(1)} %bitcast.13, bf16[64,1024]{1,0:T(8,128)(2,1)S(1)} %bitcast.19), custom_call_target="tpu_custom_call" | custom-call | flops 134217728 | bytes 2097152 | tf_op jit(solution)/shard_map/project/pallas_call | solution.py:106
  40.2 2.7 %collective-permute-done.3.refs_4_ = f32[128,512]{1,0:T(8,128)S(1)} collective-permute-done((f32[128,512]{1,0:T(8,128)S(1)}, f32[128,512]{1,0:T(8,128)S(1)}, u32[]{:S(2)}, u32[]{:S(2)}) %collective-permute-start.3) | collective-permute-done | bytes 262176 | tf_op jit(solution)/shard_map/ppermute | solution.py:220
  42.9 5.5 %collective-permute-done.5.refs_6_ = f32[128,512]{1,0:T(8,128)S(1)} collective-permute-done((f32[128,512]{1,0:T(8,128)S(1)}, f32[128,512]{1,0:T(8,128)S(1)}, u32[]{:S(2)}, u32[]{:S(2)}) %collective-permute-start.5) | collective-permute-done | bytes 262176 | tf_op jit(solution)/shard_map/ppermute | solution.py:220
  48.4 3.9 %collective-permute-start.6 = (f32[128,512]{1,0:T(8,128)S(1)}, f32[128,512]{1,0:T(8,128)S(1)}, u32[]{:S(2)}, u32[]{:S(2)}) collective-permute-start(f32[128,512]{1,0:T(8,128)S(1)} %get-tuple-element.24), channel_id=1, source_target_pairs={{0,112},{16,96},{32,80},{48,64},{64,48},{80,32},{96,16},{112,0},{1... | collective-permute-start | bytes 786440 | tf_op jit(solution)/shard_map/ppermute | solution.py:220
  52.4 7.0 %collective-permute-done.6.refs_7_ = f32[128,512]{1,0:T(8,128)S(1)} collective-permute-done((f32[128,512]{1,0:T(8,128)S(1)}, f32[128,512]{1,0:T(8,128)S(1)}, u32[]{:S(2)}, u32[]{:S(2)}) %collective-permute-start.6) | collective-permute-done | bytes 262176 | tf_op jit(solution)/shard_map/ppermute | solution.py:220
  60.2 14.6 %all_to_all.10.rows_ref = f32[16,16,128]{2,1,0:T(8,128)S(1)} all-to-all(f32[16,16,128]{2,1,0:T(8,128)S(1)} %gradient.1), channel_id=1, replica_groups={{0,16,32,48,64,80,96,112,8,24,40,56,72,88,104,120},{1,17,33,49,65,81,97..., dimensions={0} | all-to-all | bytes 262144 | tf_op jit(solution)/shard_map/all_to_all | solution.py:249
  75.9 16.9 %all_to_all.11.halves_ref = f32[16,16,512]{2,1,0:T(8,128)S(1)} all-to-all(f32[16,16,512]{2,1,0:T(8,128)S(1)} %partial_precond.1), channel_id=1, replica_groups=mesh['width'=8,'store'=16] {'store'}, dimensions={0} | all-to-all | bytes 1048576 | tf_op jit(solution)/shard_map/all_to_all | solution.py:251
  92.8 2.8 %scores.1 = (f32[16,2048]{1,0:T(8,128)S(1)}, f32[16,2048]{1,0:T(8,128)S(1)}, f32[16,2048]{1,0:T(8,128)S(1)}, f32[16,2048]{1,0:T(8,128)S(1)}, f32[16,2048]{1,0:T(...) custom-call(s32[2]{0:T(128)S(1)} %pad_add_fusion.place_ref, ...), custom_call_target="tpu_custom_call" | custom-call | tf_op jit(solution)/shard_map/scores/pallas_call | solution.py:208
  96.8 1.8 %collective-permute-start.15 = (f32[16,2048]{1,0:T(8,128)S(1)}, f32[16,2048]{1,0:T(8,128)S(1)}, u32[]{:S(2)}, u32[]{:S(2)}) collective-permute-start(f32[16,2048]{1,0:T(8,128)S(1)} %get-tuple-element.31), channel_id=1, source_target_pairs={{0,48},{16,32},{32,16},{48,0},{64,112},{80,96},{96,80},{112,64},{1... | collective-permute-start | bytes 393224 | tf_op jit(solution)/shard_map/ppermute | solution.py:220
  98.6 2.2 %collective-permute-start.16 = (f32[16,2048]{1,0:T(8,128)S(1)}, f32[16,2048]{1,0:T(8,128)S(1)}, u32[]{:S(2)}, u32[]{:S(2)}) collective-permute-start(f32[16,2048]{1,0:T(8,128)S(1)} %get-tuple-element.32), channel_id=1, source_target_pairs={{0,112},{16,96},{32,80},{48,64},{64,48},{80,32},{96,16},{112,0},{1... | collective-permute-start | bytes 393224 | tf_op jit(solution)/shard_map/ppermute | solution.py:220
  106.9 2.6 %collective-permute-done.16 = f32[16,2048]{1,0:T(8,128)S(1)} collective-permute-done((f32[16,2048]{1,0:T(8,128)S(1)}, f32[16,2048]{1,0:T(8,128)S(1)}, u32[]{:S(2)}, u32[]{:S(2)}) %collective-permute-start.16) | collective-permute-done | bytes 131104 | tf_op jit(solution)/shard_map/ppermute | solution.py:220
  110.0 2.3 %collective-permute-done.19 = f32[16,2048]{1,0:T(8,128)S(1)} collective-permute-done((f32[16,2048]{1,0:T(8,128)S(1)}, f32[16,2048]{1,0:T(8,128)S(1)}, u32[]{:S(2)}, u32[]{:S(2)}) %collective-permute-start.19) | collective-permute-done | bytes 131104 | tf_op jit(solution)/shard_map/ppermute | solution.py:220
  (57 shorter events, 16.1 us)
Async XLA Ops:
  0.0 32.3 %collective-permute-start.9 = (f32[256,512]{1,0:T(8,128)}, f32[256,512]{1,0:T(8,128)S(1)}, u32[]{:S(2)}, u32[]{:S(2)}) collective-permute-start(f32[256,512]{1,0:T(8,128)} %refs_0_.1), channel_id=1, source_target_pairs={{0,6},{1,7},{2,4},{3,5},{4,2},{5,3},{6,0},{7,1},{8,14},{9,15},{10,... | collective-permute-start | bytes 1572872 | tf_op jit(solution)/shard_map/ppermute | solution.py:220
  4.2 28.5 %collective-permute-start.8 = (f32[256,512]{1,0:T(8,128)}, f32[256,512]{1,0:T(8,128)S(1)}, u32[]{:S(2)}, u32[]{:S(2)}) collective-permute-start(f32[256,512]{1,0:T(8,128)} %refs_0_.1), channel_id=1, source_target_pairs={{0,4},{1,5},{2,6},{3,7},{4,0},{5,1},{6,2},{7,3},{8,12},{9,13},{10,... | collective-permute-start | bytes 1572872 | tf_op jit(solution)/shard_map/ppermute | solution.py:220
  4.2 33.5 %collective-permute-start.7 = (f32[256,512]{1,0:T(8,128)}, f32[256,512]{1,0:T(8,128)S(1)}, u32[]{:S(2)}, u32[]{:S(2)}) collective-permute-start(f32[256,512]{1,0:T(8,128)} %refs_0_.1), channel_id=1, source_target_pairs={{0,2},{1,3},{2,0},{3,1},{4,6},{5,7},{6,4},{7,5},{8,10},{9,11},{10,... | collective-permute-start | bytes 1572872 | tf_op jit(solution)/shard_map/ppermute | solution.py:220
  15.0 13.2 %collective-permute-start.1 = (f32[128,512]{1,0:T(8,128)S(1)}, f32[128,512]{1,0:T(8,128)S(1)}, u32[]{:S(2)}, u32[]{:S(2)}) collective-permute-start(f32[128,512]{1,0:T(8,128)S(1)} %project.7), channel_id=1, source_target_pairs={{0,32},{16,48},{32,0},{48,16},{64,96},{80,112},{96,64},{112,80},{1... | collective-permute-start | bytes 786440 | tf_op jit(solution)/shard_map/ppermute | solution.py:220
  17.9 21.6 %collective-permute-start.2 = (f32[128,512]{1,0:T(8,128)S(1)}, f32[128,512]{1,0:T(8,128)S(1)}, u32[]{:S(2)}, u32[]{:S(2)}) collective-permute-start(f32[128,512]{1,0:T(8,128)S(1)} %project.8), channel_id=1, source_target_pairs={{0,48},{16,32},{32,16},{48,0},{64,112},{80,96},{96,80},{112,64},{1... | collective-permute-start | bytes 786440 | tf_op jit(solution)/shard_map/ppermute | solution.py:220
  19.4 16.3 %slice-start = ((s8[8388608]{0:T(1024)(128)(4,1)}), s8[4194304]{0:T(1024)(128)(4,1)S(1)}, s32[]{:S(2)}) async-start(s8[8388608]{0:T(1024)(128)(4,1)} %bitcast.4), calls=%async_computation.2 | async-start | bytes 8388608
  19.4 16.3 %slice-start.2 = ((s8[8388608]{0:T(1024)(128)(4,1)}), s8[4194304]{0:T(1024)(128)(4,1)S(1)}, s32[]{:S(2)}) async-start(s8[8388608]{0:T(1024)(128)(4,1)} %bitcast.6), calls=%async_computation.4 | async-start | bytes 8388608
  28.1 11.5 %collective-permute-start.4 = (f32[128,512]{1,0:T(8,128)S(1)}, f32[128,512]{1,0:T(8,128)S(1)}, u32[]{:S(2)}, u32[]{:S(2)}) collective-permute-start(f32[128,512]{1,0:T(8,128)S(1)} %project_first.1), channel_id=1, source_target_pairs={{0,80},{16,64},{32,112},{48,96},{64,16},{80,0},{96,48},{112,32},{1... | collective-permute-start | bytes 786440 | tf_op jit(solution)/shard_map/ppermute | solution.py:220
  32.3 10.6 %collective-permute-start.3 = (f32[128,512]{1,0:T(8,128)S(1)}, f32[128,512]{1,0:T(8,128)S(1)}, u32[]{:S(2)}, u32[]{:S(2)}) collective-permute-start(f32[128,512]{1,0:T(8,128)S(1)} %get-tuple-element.22), channel_id=1, source_target_pairs={{0,64},{16,80},{32,96},{48,112},{64,0},{80,16},{96,32},{112,48},{1... | collective-permute-start | bytes 786440 | tf_op jit(solution)/shard_map/ppermute | solution.py:220
  32.6 15.8 %collective-permute-start.5 = (f32[128,512]{1,0:T(8,128)S(1)}, f32[128,512]{1,0:T(8,128)S(1)}, u32[]{:S(2)}, u32[]{:S(2)}) collective-permute-start(f32[128,512]{1,0:T(8,128)S(1)} %get-tuple-element.23), channel_id=1, source_target_pairs={{0,96},{16,112},{32,64},{48,80},{64,32},{80,48},{96,0},{112,16},{1... | collective-permute-start | bytes 786440 | tf_op jit(solution)/shard_map/ppermute | solution.py:220
  37.6 10.8 %collective-permute-start = (f32[128,512]{1,0:T(8,128)S(1)}, f32[128,512]{1,0:T(8,128)S(1)}, u32[]{:S(2)}, u32[]{:S(2)}) collective-permute-start(f32[128,512]{1,0:T(8,128)S(1)} %get-tuple-element.21), channel_id=1, source_target_pairs={{0,16},{16,0},{32,48},{48,32},{64,80},{80,64},{96,112},{112,96},{1... | collective-permute-start | bytes 786440 | tf_op jit(solution)/shard_map/ppermute | solution.py:220
  39.5 53.2 %copy-start.6 = (f32[2048,512]{1,0:T(8,128)S(1)}, f32[2048,512]{1,0:T(8,128)}, u32[]{:S(2)}) copy-start(f32[2048,512]{1,0:T(8,128)} %store_ref.1) | copy-start | bytes 12582916
  39.6 35.2 %collective-permute-start.10 = (f32[256,512]{1,0:T(8,128)S(1)}, f32[256,512]{1,0:T(8,128)S(1)}, u32[]{:S(2)}, u32[]{:S(2)}) collective-permute-start(f32[256,512]{1,0:T(8,128)S(1)} %copy-done.7), channel_id=1, source_target_pairs={{0,1},{1,0},{2,3},{3,2},{4,5},{5,4},{6,7},{7,6},{8,9},{9,8},{10,11... | collective-permute-start | bytes 1572872 | tf_op jit(solution)/shard_map/ppermute | solution.py:220
  39.7 35.1 %collective-permute-start.11 = (f32[256,512]{1,0:T(8,128)S(1)}, f32[256,512]{1,0:T(8,128)S(1)}, u32[]{:S(2)}, u32[]{:S(2)}) collective-permute-start(f32[256,512]{1,0:T(8,128)S(1)} %collective-permute-done.7.refs_2_), channel_id=1, source_target_pairs={{0,1},{1,0},{2,3},{3,2},{4,5},{5,4},{6,7},{7,6},{8,9},{9,8},{10,11... | collective-permute-start | bytes 1572872 | tf_op jit(solution)/shard_map/ppermute | solution.py:220
  42.9 31.9 %collective-permute-start.12 = (f32[256,512]{1,0:T(8,128)S(1)}, f32[256,512]{1,0:T(8,128)S(1)}, u32[]{:S(2)}, u32[]{:S(2)}) collective-permute-start(f32[256,512]{1,0:T(8,128)S(1)} %collective-permute-done.8.refs_4_), channel_id=1, source_target_pairs={{0,1},{1,0},{2,3},{3,2},{4,5},{5,4},{6,7},{7,6},{8,9},{9,8},{10,11... | collective-permute-start | bytes 1572872 | tf_op jit(solution)/shard_map/ppermute | solution.py:220
  48.4 26.4 %collective-permute-start.13 = (f32[256,512]{1,0:T(8,128)S(1)}, f32[256,512]{1,0:T(8,128)S(1)}, u32[]{:S(2)}, u32[]{:S(2)}) collective-permute-start(f32[256,512]{1,0:T(8,128)S(1)} %collective-permute-done.9.refs_6_), channel_id=1, source_target_pairs={{0,1},{1,0},{2,3},{3,2},{4,5},{5,4},{6,7},{7,6},{8,9},{9,8},{10,11... | collective-permute-start | bytes 1572872 | tf_op jit(solution)/shard_map/ppermute | solution.py:220
  48.4 10.9 %collective-permute-start.6 = (f32[128,512]{1,0:T(8,128)S(1)}, f32[128,512]{1,0:T(8,128)S(1)}, u32[]{:S(2)}, u32[]{:S(2)}) collective-permute-start(f32[128,512]{1,0:T(8,128)S(1)} %get-tuple-element.24), channel_id=1, source_target_pairs={{0,112},{16,96},{32,80},{48,64},{64,48},{80,32},{96,16},{112,0},{1... | collective-permute-start | bytes 786440 | tf_op jit(solution)/shard_map/ppermute | solution.py:220
  95.6 8.9 %collective-permute-start.14 = (f32[16,2048]{1,0:T(8,128)S(1)}, f32[16,2048]{1,0:T(8,128)S(1)}, u32[]{:S(2)}, u32[]{:S(2)}) collective-permute-start(f32[16,2048]{1,0:T(8,128)S(1)} %get-tuple-element.30), channel_id=1, source_target_pairs={{0,80},{16,64},{32,112},{48,96},{64,16},{80,0},{96,48},{112,32},{1... | collective-permute-start | bytes 393224 | tf_op jit(solution)/shard_map/ppermute | solution.py:220
  96.8 9.0 %collective-permute-start.15 = (f32[16,2048]{1,0:T(8,128)S(1)}, f32[16,2048]{1,0:T(8,128)S(1)}, u32[]{:S(2)}, u32[]{:S(2)}) collective-permute-start(f32[16,2048]{1,0:T(8,128)S(1)} %get-tuple-element.31), channel_id=1, source_target_pairs={{0,48},{16,32},{32,16},{48,0},{64,112},{80,96},{96,80},{112,64},{1... | collective-permute-start | bytes 393224 | tf_op jit(solution)/shard_map/ppermute | solution.py:220
  98.6 10.9 %collective-permute-start.16 = (f32[16,2048]{1,0:T(8,128)S(1)}, f32[16,2048]{1,0:T(8,128)S(1)}, u32[]{:S(2)}, u32[]{:S(2)}) collective-permute-start(f32[16,2048]{1,0:T(8,128)S(1)} %get-tuple-element.32), channel_id=1, source_target_pairs={{0,112},{16,96},{32,80},{48,64},{64,48},{80,32},{96,16},{112,0},{1... | collective-permute-start | bytes 393224 | tf_op jit(solution)/shard_map/ppermute | solution.py:220
  100.8 8.7 %collective-permute-start.17 = (f32[16,2048]{1,0:T(8,128)S(1)}, f32[16,2048]{1,0:T(8,128)S(1)}, u32[]{:S(2)}, u32[]{:S(2)}) collective-permute-start(f32[16,2048]{1,0:T(8,128)S(1)} %get-tuple-element.33), channel_id=1, source_target_pairs={{0,16},{16,0},{32,48},{48,32},{64,80},{80,64},{96,112},{112,96},{1... | collective-permute-start | bytes 393224 | tf_op jit(solution)/shard_map/ppermute | solution.py:220
  102.1 7.9 %collective-permute-start.18 = (f32[16,2048]{1,0:T(8,128)S(1)}, f32[16,2048]{1,0:T(8,128)S(1)}, u32[]{:S(2)}, u32[]{:S(2)}) collective-permute-start(f32[16,2048]{1,0:T(8,128)S(1)} %get-tuple-element.34), channel_id=1, source_target_pairs={{0,64},{16,80},{32,96},{48,112},{64,0},{80,16},{96,32},{112,48},{1... | collective-permute-start | bytes 393224 | tf_op jit(solution)/shard_map/ppermute | solution.py:220
  104.5 7.9 %collective-permute-start.19 = (f32[16,2048]{1,0:T(8,128)S(1)}, f32[16,2048]{1,0:T(8,128)S(1)}, u32[]{:S(2)}, u32[]{:S(2)}) collective-permute-start(f32[16,2048]{1,0:T(8,128)S(1)} %get-tuple-element.35), channel_id=1, source_target_pairs={{0,96},{16,112},{32,64},{48,80},{64,32},{80,48},{96,0},{112,16},{1... | collective-permute-start | bytes 393224 | tf_op jit(solution)/shard_map/ppermute | solution.py:220
  105.7 6.6 %collective-permute-start.20 = (f32[16,2048]{1,0:T(8,128)S(1)}, f32[16,2048]{1,0:T(8,128)S(1)}, u32[]{:S(2)}, u32[]{:S(2)}) collective-permute-start(f32[16,2048]{1,0:T(8,128)S(1)} %get-tuple-element.36), channel_id=1, source_target_pairs={{0,32},{16,48},{32,0},{48,16},{64,96},{80,112},{96,64},{112,80},{1... | collective-permute-start | bytes 393224 | tf_op jit(solution)/shard_map/ppermute | solution.py:220
  (9 other events, 67.8 us)

commit v2 on v1

--- a/solution.py
+++ b/solution.py
@@ -151,19 +151,16 @@
 
 def partial_kernel(rows_ref, *refs):
     *fisher_refs, result_ref = refs
-    high, low = split(rows_ref[...])
     total = None
     for i, fisher_ref in enumerate(fisher_refs):
+        rows = jnp.concatenate([rows_ref[:, 2 * i, :], rows_ref[:, 2 * i + 1, :]], axis=1)
+        high, low = split(rows)
         f_high, f_low = split(fisher_ref[...])
-        for side in range(2):
-            rows = 2 * i + side
-            span = slice(side * 128, (side + 1) * 128)
-            a_high, a_low = high[:, rows, :], low[:, rows, :]
-            term = dot(a_high, f_high[span], NN) + (
-                dot(a_high, f_low[span], NN) + dot(a_low, f_high[span], NN)
-            )
-            total = term if total is None else total + term
-    for i in range(STORE):
+        half = rows.shape[0]
+        wide = dot(jnp.concatenate([high, low], axis=0), f_high, NN)
+        term = wide[:half] + (wide[half:] + dot(high, f_low, NN))
+        total = term if total is None else total + term
+    for i in range(STORE // 2):
         result_ref[i] = total
 
 
@@ -171,7 +168,7 @@
     columns = fisher[0].shape[1]
     return pl.pallas_call(
         partial_kernel,
-        out_shape=jax.ShapeDtypeStruct((STORE, 2 * WIDTH, columns), jnp.float32),
+        out_shape=jax.ShapeDtypeStruct((STORE // 2, 2 * WIDTH, columns), jnp.float32),
         in_specs=[VMEM] * (1 + len(fisher)),
         out_specs=VMEM,
         compiler_params=limit(10),
@@ -179,49 +176,67 @@
     )(rows, *fisher)
 
 
-def score_kernel(place_ref, halves_ref, store_ref, *refs):
-    *result_refs, p_high, p_low = refs
+def split_kernel(store_ref, high_ref, low_ref):
+    high_ref[...], low_ref[...] = split(store_ref[...])
+
+
+def split_store(store):
+    half = jax.ShapeDtypeStruct(store.shape, jnp.bfloat16)
+    return pl.pallas_call(
+        split_kernel,
+        out_shape=(half, half),
+        in_specs=[VMEM],
+        out_specs=(VMEM, VMEM),
+        compiler_params=limit(12),
+        name="split_store",
+    )(store)
+
+
+def score_kernel(place_ref, own_ref, other_ref, high_ref, low_ref, *refs):
+    *result_refs, parts = refs
     rows = 8
+    half = 2 * WIDTH * rows
     for k in range(WIDTH):
         owner = place_ref[0] ^ k
+        z = owner & 3
         offset = pl.ds(pl.multiple_of((owner >> 2) * rows, rows), rows)
-        for core in range(2):
-            near = ((2 * owner) & (NEAR - 1)) + core
-            block = halves_ref[near, offset, :] + halves_ref[NEAR + near, offset, :]
-            span = slice((2 * k + core) * rows, (2 * k + core + 1) * rows)
-            p_high[span, :] = block.astype(jnp.bfloat16).astype(jnp.float32)
-            p_low[span, :] = block - p_high[span, :]
-    a_high = p_high[...].astype(jnp.bfloat16)
-    a_low = p_low[...].astype(jnp.bfloat16)
+        for swap, halves_ref in enumerate((own_ref, other_ref)):
+            core = (place_ref[1] & 1) ^ swap
+            block = halves_ref[z, offset, :] + halves_ref[4 + z, offset, :]
+            start = pl.multiple_of((2 * k + core) * rows, rows)
+            high = block.astype(jnp.bfloat16).astype(jnp.float32)
+            parts[pl.ds(start, rows), :] = high
+            parts[pl.ds(start + half, rows), :] = block - high
+    both = parts[...].astype(jnp.bfloat16)
     width = 512
-    for n in range(store_ref.shape[0] // width):
+    for n in range(high_ref.shape[0] // width):
         span = slice(n * width, (n + 1) * width)
-        b_high, b_low = split(store_ref[span, :])
-        total = dot(a_high, b_high, NT) + (dot(a_high, b_low, NT) + dot(a_low, b_high, NT))
+        wide = dot(both, high_ref[span, :], NT)
+        total = wide[:half] + (wide[half:] + dot(both[:half], low_ref[span, :], NT))
         for k in range(WIDTH):
             result_refs[k][:, span] = total[16 * k : 16 * (k + 1), :]
 
 
-def scores(place, halves, store):
-    examples, columns = store.shape
+def scores(place, own, other, high, low):
+    examples, columns = high.shape
     block = jax.ShapeDtypeStruct((16, examples), jnp.float32)
     return pl.pallas_call(
         score_kernel,
         out_shape=(block,) * WIDTH,
-        in_specs=[SMEM, VMEM, VMEM],
+        in_specs=[SMEM, VMEM, VMEM, VMEM, VMEM],
         out_specs=(VMEM,) * WIDTH,
-        scratch_shapes=[pltpu.VMEM((128, columns), jnp.float32)] * 2,
+        scratch_shapes=[pltpu.VMEM((256, columns), jnp.float32)],
         compiler_params=limit(12),
         name="scores",
-    )(place, halves, store)
+    )(place, own, other, high, low)
 
 
 def exchange(x, axis, k, size):
     return lax.ppermute(x, axis, [(i, i ^ k) for i in range(size)])
 
 
-ORDER = (5, 3, 7, 1, 4, 6, 2)
-GROUPS = (((5,), 4), ((3,), 2), ((7, 1), 6), ((4, 6), 0), ((2,), 0), ((0,), 0))
+ORDER = (5, 4, 3, 7, 6, 2, 1)
+GROUPS = (((5,), (4, 2)), ((4,), (6,)), ((3, 7), ()), ((6, 2), ()), ((1,), ()), ((0,), ()))
 
 
 def body(activations, out_grads, proj_in, proj_out, fisher_inv, grad_store):
@@ -229,18 +244,20 @@
     proj_in_t, proj_out_t = proj_in.T, proj_out.T
     weights = (activations, out_grads, proj_in_t, proj_out_t)
     parts, fisher = {}, {0: fisher_inv}
-    for n, (group, far) in enumerate(GROUPS):
+    for n, (group, around) in enumerate(GROUPS):
         if n:
             projected = project(group, place, *weights)
         else:
             projected = (project_first(group[0], place, *weights),)
         for k, part in zip(group, projected, strict=True):
             parts[k] = exchange(part, "width", k, WIDTH) if k else part
-        if far:
+        for far in around:
             fisher[far] = exchange(fisher_inv, "store", far, STORE)
     last, *blocks = lax.optimization_barrier((parts[0], *(fisher[k] for k in (0, 2, 4, 6))))
     for k, block in zip((0, 2, 4, 6), blocks, strict=True):
         fisher[k + 1] = exchange(block, "store", 1, STORE)
+    store, _ = lax.optimization_barrier((grad_store, parts[0]))
+    high, low = split_store(store)
     outgoing = gradient(place, [parts[k] for k in range(WIDTH)])
     groups = [
         [(side * NEAR + i) * WIDTH + w for side in range(2) for w in range(WIDTH)]
@@ -248,8 +265,9 @@
     ]
     rows = lax.all_to_all(outgoing, ("store", "width"), 0, 0, axis_index_groups=groups)
     halves = partial_precond(rows, [fisher[i] for i in range(NEAR)])
-    halves = lax.all_to_all(halves, "store", 0, 0)
-    blocks = scores(place, halves, grad_store)
+    cores = [list(range(core, STORE, 2)) for core in range(2)]
+    halves = lax.all_to_all(halves, "store", 0, 0, axis_index_groups=cores)
+    blocks = scores(place, halves, exchange(halves, "store", 1, STORE), high, low)
     total = blocks[0]
     for block in [exchange(blocks[k], "width", k, WIDTH) for k in ORDER]:
         total = total + block

time: 114 us -> 109 us (0.956)
  waiting for transfers between devices: 25.2 us -> 32.9 us
  blocking collectives: 31.5 us -> 25.4 us
  starting transfers between devices: 30.8 us -> 25.5 us
    ppermute x21 -> x22, waiting for transfers between devices: 25.2 us -> 32.9 us  [exchange(): return lax.ppermute(x, axis, [(i, i ^ k) for i in range(size)])]
    ppermute x21 -> x22, starting transfers between devices: 30.8 us -> 25.5 us  [exchange(): return lax.ppermute(x, axis, [(i, i ^ k) for i in range(size)])]
    all_to_all x1, blocking collectives: 16.9 us -> 13.5 us  [body(): halves = lax.all_to_all(halves, 'store', 0, 0, axis_index_groups=cores)]
    all_to_all x1, blocking collectives: 14.6 us -> 11.9 us  [body(): lax.all_to_all(outgoing, ('store', 'width'), 0, 0, axis_index_groups=groups)]
  transfers between devices with their start and end apart: 21 -> 22, of which waited for: 9 -> 10; matrix products, arithmetic and copies ran while one was open for 0% -> 0% of each run, Pallas kernels for 11% -> 12%
where the time goes in v2:
time: 109 us
  waiting for transfers between devices  32.9 us (30%)
  starting transfers between devices  25.5 us (23%)
  blocking collectives  25.4 us (23%)
  Pallas kernels  15.7 us (14%)
  local copies, waits for them, and re-layouts  8.62 us (8%)
    ppermute x22, waiting for transfers between devices, exchange(): return lax.ppermute(x, axis, [(i, i ^ k) for i in range(size)])  32.9 us
    ppermute x22, starting transfers between devices, exchange(): return lax.ppermute(x, axis, [(i, i ^ k) for i in range(size)])  25.5 us
    all_to_all x1, blocking collectives, body(): halves = lax.all_to_all(halves, 'store', 0, 0, axis_index_groups=cores)  13.5 us
    all_to_all x1, blocking collectives, body(): lax.all_to_all(outgoing, ('store', 'width'), 0, 0, axis_index_groups=groups)  11.9 us
    unnamed x24, local copies, waits for them, and re-layouts  8.62 us
    pallas_call x5, Pallas kernels, project(): pl.pallas_call(functools.partial(project_kernel, group), out_shape=(part,...  7.74 us
    pallas_call x1, Pallas kernels, project_first(): pl.pallas_call(functools.partial(project_first_kernel, k), out_shape=jax....  3.51 us
  transfers between devices with their start and end apart: 22, of which 10 were waited for; matrix products, arithmetic and copies ran while one was open for 0% of the time, Pallas kernels for 12%

profile of v2, /device:TPU:0, one launch (start us, length us, event | category | flops | bytes accessed | tf_op | source)
XLA Modules:
  0.0 109.0 jit_solution(1476489744373097921)
XLA Ops:
  0.0 4.1 %collective-permute-start.9 = (f32[256,512]{1,0:T(8,128)}, f32[256,512]{1,0:T(8,128)S(1)}, u32[]{:S(2)}, u32[]{:S(2)}) collective-permute-start(f32[256,512]{1,0:T(8,128)} %refs_0_.1), channel_id=1, source_target_pairs={{0,6},{1,7},{2,4},{3,5},{4,2},{5,3},{6,0},{7,1},{8,14},{9,15},{10,... | collective-permute-start | bytes 1572872 | tf_op jit(solution)/shard_map/ppermute | solution.py:235
  5.1 3.4 %copy-done = bf16[8,512,1024]{2,1,0:T(8,128)(2,1)S(1)} copy-done((bf16[8,512,1024]{2,1,0:T(8,128)(2,1)S(1)}, bf16[8,512,1024]{2,1,0:T(8,128)(2,1)}, u32[]{:S(2)}) %copy-start) | copy-done | bytes 8388632
  8.5 3.4 %copy-done.1 = bf16[8,512,1024]{2,1,0:T(8,128)(2,1)S(1)} copy-done((bf16[8,512,1024]{2,1,0:T(8,128)(2,1)S(1)}, bf16[8,512,1024]{2,1,0:T(8,128)(2,1)}, u32[]{:S(2)}) %copy-start.1) | copy-done | bytes 8388632
  13.7 1.3 %project.6 = f32[128,512]{1,0:T(8,128)S(1)} custom-call(s32[2]{0:T(128)S(1)} %pad_add_fusion.place_ref, bf16[8,512,1024]{2,1,0:T(8,128)(2,1)S(1)} %copy-done, bf16[8,512,1024]{2,1,0:T(8,128)(2,1)S(1)} %copy-done.1, bf16[64,1024]{1,0:T(8,128)(2,1)S(1)} %bitcast.9, bf16[64,1024]{1,0:T(8,128)(2,1)S(1)} %bitcast.15), custom_call_target="tpu_custom_call" | custom-call | flops 134217728 | bytes 2097152 | tf_op jit(solution)/shard_map/project/pallas_call | solution.py:106
  15.0 1.6 %collective-permute-start = (f32[128,512]{1,0:T(8,128)S(1)}, f32[128,512]{1,0:T(8,128)S(1)}, u32[]{:S(2)}, u32[]{:S(2)}) collective-permute-start(f32[128,512]{1,0:T(8,128)S(1)} %project.6), channel_id=1, source_target_pairs={{0,16},{16,0},{32,48},{48,32},{64,80},{80,64},{96,112},{112,96},{1... | collective-permute-start | bytes 786440 | tf_op jit(solution)/shard_map/ppermute | solution.py:235
  17.8 3.3 %collective-permute-start.3 = (f32[128,512]{1,0:T(8,128)S(1)}, f32[128,512]{1,0:T(8,128)S(1)}, u32[]{:S(2)}, u32[]{:S(2)}) collective-permute-start(f32[128,512]{1,0:T(8,128)S(1)} %project.9), channel_id=1, source_target_pairs={{0,64},{16,80},{32,96},{48,112},{64,0},{80,16},{96,32},{112,48},{1... | collective-permute-start | bytes 786440 | tf_op jit(solution)/shard_map/ppermute | solution.py:235
  21.1 1.9 %project.8 = (f32[128,512]{1,0:T(8,128)S(1)}, f32[128,512]{1,0:T(8,128)S(1)}) custom-call(s32[2]{0:T(128)S(1)} %pad_add_fusion.place_ref, bf16[8,512,1024]{2,1,0:T(8,128)(2,1)S(1)} %copy-done, bf16[8,512,1024]{2,1,0:T(8,128)(2,1)S(1)} %copy-done.1, bf16[64,1024]{1,0:T(8,128)(2,1)S(1)} %bitcast.11, bf16[64,1024]{1,0:T(8,128)(2,1)S(1)} %bitcast.17), custom_call_target="tpu_custom_call" | custom-call | flops 268435456 | bytes 4194304 | tf_op jit(solution)/shard_map/project/pallas_call | solution.py:106
  23.1 3.5 %project_first.1 = f32[128,512]{1,0:T(8,128)S(1)} custom-call(s32[2]{0:T(128)S(1)} %pad_add_fusion.place_ref, bf16[8,512,1024]{2,1,0:T(8,128)(2,1)} %act_ref.11, bf16[8,512,1024]{2,1,0:T(8,128)(2,1)} %grad_ref.11, bf16[64,1024]{1,0:T(8,128)(2,1)} %bitcast.8, bf16[64,1024]{1,0:T(8,128)(2,1)} %bitcast.14), custom_call_target="tpu_custom_call" | custom-call | flops 134217728 | bytes 2097152 | tf_op jit(solution)/shard_map/project_first/pallas_call | solution.py:71
  27.5 2.5 %collective-permute-start.2 = (f32[128,512]{1,0:T(8,128)S(1)}, f32[128,512]{1,0:T(8,128)S(1)}, u32[]{:S(2)}, u32[]{:S(2)}) collective-permute-start(f32[128,512]{1,0:T(8,128)S(1)} %get-tuple-element.25), channel_id=1, source_target_pairs={{0,48},{16,32},{32,16},{48,0},{64,112},{80,96},{96,80},{112,64},{1... | collective-permute-start | bytes 786440 | tf_op jit(solution)/shard_map/ppermute | solution.py:235
  30.0 2.2 %collective-permute-start.6 = (f32[128,512]{1,0:T(8,128)S(1)}, f32[128,512]{1,0:T(8,128)S(1)}, u32[]{:S(2)}, u32[]{:S(2)}) collective-permute-start(f32[128,512]{1,0:T(8,128)S(1)} %get-tuple-element.27), channel_id=1, source_target_pairs={{0,112},{16,96},{32,80},{48,64},{64,48},{80,32},{96,16},{112,0},{1... | collective-permute-start | bytes 786440 | tf_op jit(solution)/shard_map/ppermute | solution.py:235
  32.2 1.9 %project.7 = (f32[128,512]{1,0:T(8,128)S(1)}, f32[128,512]{1,0:T(8,128)S(1)}) custom-call(s32[2]{0:T(128)S(1)} %pad_add_fusion.place_ref, bf16[8,512,1024]{2,1,0:T(8,128)(2,1)S(1)} %bitcast.5, bf16[8,512,1024]{2,1,0:T(8,128)(2,1)S(1)} %bitcast.7, bf16[64,1024]{1,0:T(8,128)(2,1)S(1)} %bitcast.12, bf16[64,1024]{1,0:T(8,128)(2,1)S(1)} %bitcast.18), custom_call_target="tpu_custom_call" | custom-call | flops 268435456 | bytes 4194304 | tf_op jit(solution)/shard_map/project/pallas_call | solution.py:106
  34.9 1.3 %project.5.refs_0_ = f32[128,512]{1,0:T(8,128)S(1)} custom-call(s32[2]{0:T(128)S(1)} %pad_add_fusion.place_ref, bf16[8,512,1024]{2,1,0:T(8,128)(2,1)S(1)} %bitcast.5, bf16[8,512,1024]{2,1,0:T(8,128)(2,1)S(1)} %bitcast.7, bf16[64,1024]{1,0:T(8,128)(2,1)S(1)} %bitcast.13, bf16[64,1024]{1,0:T(8,128)(2,1)S(1)} %bitcast.19), custom_call_target="tpu_custom_call" | custom-call | flops 134217728 | bytes 2097152 | tf_op jit(solution)/shard_map/project/pallas_call | solution.py:106
  36.4 2.0 %collective-permute-done.4.refs_5_ = f32[128,512]{1,0:T(8,128)S(1)} collective-permute-done((f32[128,512]{1,0:T(8,128)S(1)}, f32[128,512]{1,0:T(8,128)S(1)}, u32[]{:S(2)}, u32[]{:S(2)}) %collective-permute-start.4) | collective-permute-done | bytes 262176 | tf_op jit(solution)/shard_map/ppermute | solution.py:235
  38.4 3.9 %collective-permute-done.2.refs_3_ = f32[128,512]{1,0:T(8,128)S(1)} collective-permute-done((f32[128,512]{1,0:T(8,128)S(1)}, f32[128,512]{1,0:T(8,128)S(1)}, u32[]{:S(2)}, u32[]{:S(2)}) %collective-permute-start.2) | collective-permute-done | bytes 262176 | tf_op jit(solution)/shard_map/ppermute | solution.py:235
  42.3 4.8 %collective-permute-done.6.refs_7_ = f32[128,512]{1,0:T(8,128)S(1)} collective-permute-done((f32[128,512]{1,0:T(8,128)S(1)}, f32[128,512]{1,0:T(8,128)S(1)}, u32[]{:S(2)}, u32[]{:S(2)}) %collective-permute-start.6) | collective-permute-done | bytes 262176 | tf_op jit(solution)/shard_map/ppermute | solution.py:235
  47.8 9.2 %collective-permute-done.5.refs_6_ = f32[128,512]{1,0:T(8,128)S(1)} collective-permute-done((f32[128,512]{1,0:T(8,128)S(1)}, f32[128,512]{1,0:T(8,128)S(1)}, u32[]{:S(2)}, u32[]{:S(2)}) %collective-permute-start.5) | collective-permute-done | bytes 262176 | tf_op jit(solution)/shard_map/ppermute | solution.py:235
  57.9 11.9 %all_to_all.10.rows_ref = f32[16,16,128]{2,1,0:T(8,128)S(1)} all-to-all(f32[16,16,128]{2,1,0:T(8,128)S(1)} %gradient.1), channel_id=1, replica_groups={{0,16,32,48,64,80,96,112,8,24,40,56,72,88,104,120},{1,17,33,49,65,81,97..., dimensions={0} | all-to-all | bytes 262144 | tf_op jit(solution)/shard_map/all_to_all | solution.py:266
  70.8 13.5 %all_to_all.11.own_ref = f32[8,16,512]{2,1,0:T(8,128)S(1)} all-to-all(f32[8,16,512]{2,1,0:T(8,128)S(1)} %partial_precond.1), channel_id=1, replica_groups={{0,2,4,6,8,10,12,14},{1,3,5,7,9,11,13,15},{16,18,20,22,24,26,28,30},{17..., dimensions={0} | all-to-all | bytes 524288 | tf_op jit(solution)/shard_map/all_to_all | solution.py:269
  85.8 1.9 %scores.1 = (f32[16,2048]{1,0:T(8,128)S(1)}, f32[16,2048]{1,0:T(8,128)S(1)}, f32[16,2048]{1,0:T(8,128)S(1)}, f32[16,2048]{1,0:T(8,128)S(1)}, f32[16,2048]{1,0:T(...) custom-call(s32[2]{0:T(128)S(1)} %pad_add_fusion.place_ref, ...), custom_call_target="tpu_custom_call" | custom-call | tf_op jit(solution)/shard_map/scores/pallas_call | solution.py:223
  88.9 2.6 %collective-permute-start.16 = (f32[16,2048]{1,0:T(8,128)S(1)}, f32[16,2048]{1,0:T(8,128)S(1)}, u32[]{:S(2)}, u32[]{:S(2)}) collective-permute-start(f32[16,2048]{1,0:T(8,128)S(1)} %get-tuple-element.37), channel_id=1, source_target_pairs={{0,64},{16,80},{32,96},{48,112},{64,0},{80,16},{96,32},{112,48},{1... | collective-permute-start | bytes 393224 | tf_op jit(solution)/shard_map/ppermute | solution.py:235
  93.9 2.0 %collective-permute-start.19 = (f32[16,2048]{1,0:T(8,128)S(1)}, f32[16,2048]{1,0:T(8,128)S(1)}, u32[]{:S(2)}, u32[]{:S(2)}) collective-permute-start(f32[16,2048]{1,0:T(8,128)S(1)} %get-tuple-element.40), channel_id=1, source_target_pairs={{0,96},{16,112},{32,64},{48,80},{64,32},{80,48},{96,0},{112,16},{1... | collective-permute-start | bytes 393224 | tf_op jit(solution)/shard_map/ppermute | solution.py:235
  97.2 6.1 %collective-permute-done.16 = f32[16,2048]{1,0:T(8,128)S(1)} collective-permute-done((f32[16,2048]{1,0:T(8,128)S(1)}, f32[16,2048]{1,0:T(8,128)S(1)}, u32[]{:S(2)}, u32[]{:S(2)}) %collective-permute-start.16) | collective-permute-done | bytes 131104 | tf_op jit(solution)/shard_map/ppermute | solution.py:235
  103.5 1.5 %collective-permute-done.19 = f32[16,2048]{1,0:T(8,128)S(1)} collective-permute-done((f32[16,2048]{1,0:T(8,128)S(1)}, f32[16,2048]{1,0:T(8,128)S(1)}, u32[]{:S(2)}, u32[]{:S(2)}) %collective-permute-start.19) | collective-permute-done | bytes 131104 | tf_op jit(solution)/shard_map/ppermute | solution.py:235
  105.0 3.3 %collective-permute-done.21 = f32[16,2048]{1,0:T(8,128)S(1)} collective-permute-done((f32[16,2048]{1,0:T(8,128)S(1)}, f32[16,2048]{1,0:T(8,128)S(1)}, u32[]{:S(2)}, u32[]{:S(2)}) %collective-permute-start.21) | collective-permute-done | bytes 131104 | tf_op jit(solution)/shard_map/ppermute | solution.py:235
  (60 shorter events, 15.7 us)
Async XLA Ops:
  0.0 27.5 %collective-permute-start.9 = (f32[256,512]{1,0:T(8,128)}, f32[256,512]{1,0:T(8,128)S(1)}, u32[]{:S(2)}, u32[]{:S(2)}) collective-permute-start(f32[256,512]{1,0:T(8,128)} %refs_0_.1), channel_id=1, source_target_pairs={{0,6},{1,7},{2,4},{3,5},{4,2},{5,3},{6,0},{7,1},{8,14},{9,15},{10,... | collective-permute-start | bytes 1572872 | tf_op jit(solution)/shard_map/ppermute | solution.py:235
  4.2 25.9 %collective-permute-start.8 = (f32[256,512]{1,0:T(8,128)}, f32[256,512]{1,0:T(8,128)S(1)}, u32[]{:S(2)}, u32[]{:S(2)}) collective-permute-start(f32[256,512]{1,0:T(8,128)} %refs_0_.1), channel_id=1, source_target_pairs={{0,4},{1,5},{2,6},{3,7},{4,0},{5,1},{6,2},{7,3},{8,12},{9,13},{10,... | collective-permute-start | bytes 1572872 | tf_op jit(solution)/shard_map/ppermute | solution.py:235
  4.2 30.0 %collective-permute-start.7 = (f32[256,512]{1,0:T(8,128)}, f32[256,512]{1,0:T(8,128)S(1)}, u32[]{:S(2)}, u32[]{:S(2)}) collective-permute-start(f32[256,512]{1,0:T(8,128)} %refs_0_.1), channel_id=1, source_target_pairs={{0,2},{1,3},{2,0},{3,1},{4,6},{5,7},{6,4},{7,5},{8,10},{9,11},{10,... | collective-permute-start | bytes 1572872 | tf_op jit(solution)/shard_map/ppermute | solution.py:235
  15.0 11.6 %collective-permute-start = (f32[128,512]{1,0:T(8,128)S(1)}, f32[128,512]{1,0:T(8,128)S(1)}, u32[]{:S(2)}, u32[]{:S(2)}) collective-permute-start(f32[128,512]{1,0:T(8,128)S(1)} %project.6), channel_id=1, source_target_pairs={{0,16},{16,0},{32,48},{48,32},{64,80},{80,64},{96,112},{112,96},{1... | collective-permute-start | bytes 786440 | tf_op jit(solution)/shard_map/ppermute | solution.py:235
  17.8 18.4 %collective-permute-start.3 = (f32[128,512]{1,0:T(8,128)S(1)}, f32[128,512]{1,0:T(8,128)S(1)}, u32[]{:S(2)}, u32[]{:S(2)}) collective-permute-start(f32[128,512]{1,0:T(8,128)S(1)} %project.9), channel_id=1, source_target_pairs={{0,64},{16,80},{32,96},{48,112},{64,0},{80,16},{96,32},{112,48},{1... | collective-permute-start | bytes 786440 | tf_op jit(solution)/shard_map/ppermute | solution.py:235
  21.1 11.1 %slice-start.2 = ((s8[8388608]{0:T(1024)(128)(4,1)}), s8[4194304]{0:T(1024)(128)(4,1)S(1)}, s32[]{:S(2)}) async-start(s8[8388608]{0:T(1024)(128)(4,1)} %bitcast.6), calls=%async_computation.4 | async-start | bytes 8388608
  26.6 11.8 %collective-permute-start.4 = (f32[128,512]{1,0:T(8,128)S(1)}, f32[128,512]{1,0:T(8,128)S(1)}, u32[]{:S(2)}, u32[]{:S(2)}) collective-permute-start(f32[128,512]{1,0:T(8,128)S(1)} %project_first.1), channel_id=1, source_target_pairs={{0,80},{16,64},{32,112},{48,96},{64,16},{80,0},{96,48},{112,32},{1... | collective-permute-start | bytes 786440 | tf_op jit(solution)/shard_map/ppermute | solution.py:235
  27.5 14.8 %collective-permute-start.2 = (f32[128,512]{1,0:T(8,128)S(1)}, f32[128,512]{1,0:T(8,128)S(1)}, u32[]{:S(2)}, u32[]{:S(2)}) collective-permute-start(f32[128,512]{1,0:T(8,128)S(1)} %get-tuple-element.25), channel_id=1, source_target_pairs={{0,48},{16,32},{32,16},{48,0},{64,112},{80,96},{96,80},{112,64},{1... | collective-permute-start | bytes 786440 | tf_op jit(solution)/shard_map/ppermute | solution.py:235
  30.0 17.1 %collective-permute-start.6 = (f32[128,512]{1,0:T(8,128)S(1)}, f32[128,512]{1,0:T(8,128)S(1)}, u32[]{:S(2)}, u32[]{:S(2)}) collective-permute-start(f32[128,512]{1,0:T(8,128)S(1)} %get-tuple-element.27), channel_id=1, source_target_pairs={{0,112},{16,96},{32,80},{48,64},{64,48},{80,32},{96,16},{112,0},{1... | collective-permute-start | bytes 786440 | tf_op jit(solution)/shard_map/ppermute | solution.py:235
  34.2 12.9 %collective-permute-start.1 = (f32[128,512]{1,0:T(8,128)S(1)}, f32[128,512]{1,0:T(8,128)S(1)}, u32[]{:S(2)}, u32[]{:S(2)}) collective-permute-start(f32[128,512]{1,0:T(8,128)S(1)} %get-tuple-element.24), channel_id=1, source_target_pairs={{0,32},{16,48},{32,0},{48,16},{64,96},{80,112},{96,64},{112,80},{1... | collective-permute-start | bytes 786440 | tf_op jit(solution)/shard_map/ppermute | solution.py:235
  36.2 48.0 %copy-start.6 = (f32[2048,512]{1,0:T(8,128)S(1)}, f32[2048,512]{1,0:T(8,128)}, u32[]{:S(2)}) copy-start(f32[2048,512]{1,0:T(8,128)} %store_ref) | copy-start | bytes 12582916
  36.3 33.6 %collective-permute-start.10 = (f32[256,512]{1,0:T(8,128)S(1)}, f32[256,512]{1,0:T(8,128)S(1)}, u32[]{:S(2)}, u32[]{:S(2)}) collective-permute-start(f32[256,512]{1,0:T(8,128)S(1)} %copy-done.7), channel_id=1, source_target_pairs={{0,1},{1,0},{2,3},{3,2},{4,5},{5,4},{6,7},{7,6},{8,9},{9,8},{10,11... | collective-permute-start | bytes 1572872 | tf_op jit(solution)/shard_map/ppermute | solution.py:235
  38.4 31.5 %collective-permute-start.11 = (f32[256,512]{1,0:T(8,128)S(1)}, f32[256,512]{1,0:T(8,128)S(1)}, u32[]{:S(2)}, u32[]{:S(2)}) collective-permute-start(f32[256,512]{1,0:T(8,128)S(1)} %collective-permute-done.7.refs_2_), channel_id=1, source_target_pairs={{0,1},{1,0},{2,3},{3,2},{4,5},{5,4},{6,7},{7,6},{8,9},{9,8},{10,11... | collective-permute-start | bytes 1572872 | tf_op jit(solution)/shard_map/ppermute | solution.py:235
  42.3 27.6 %collective-permute-start.12 = (f32[256,512]{1,0:T(8,128)S(1)}, f32[256,512]{1,0:T(8,128)S(1)}, u32[]{:S(2)}, u32[]{:S(2)}) collective-permute-start(f32[256,512]{1,0:T(8,128)S(1)} %collective-permute-done.8.refs_4_), channel_id=1, source_target_pairs={{0,1},{1,0},{2,3},{3,2},{4,5},{5,4},{6,7},{7,6},{8,9},{9,8},{10,11... | collective-permute-start | bytes 1572872 | tf_op jit(solution)/shard_map/ppermute | solution.py:235
  47.1 22.8 %collective-permute-start.13 = (f32[256,512]{1,0:T(8,128)S(1)}, f32[256,512]{1,0:T(8,128)S(1)}, u32[]{:S(2)}, u32[]{:S(2)}) collective-permute-start(f32[256,512]{1,0:T(8,128)S(1)} %collective-permute-done.9.refs_6_), channel_id=1, source_target_pairs={{0,1},{1,0},{2,3},{3,2},{4,5},{5,4},{6,7},{7,6},{8,9},{9,8},{10,11... | collective-permute-start | bytes 1572872 | tf_op jit(solution)/shard_map/ppermute | solution.py:235
  47.1 9.9 %collective-permute-start.5 = (f32[128,512]{1,0:T(8,128)S(1)}, f32[128,512]{1,0:T(8,128)S(1)}, u32[]{:S(2)}, u32[]{:S(2)}) collective-permute-start(f32[128,512]{1,0:T(8,128)S(1)} %get-tuple-element.26), channel_id=1, source_target_pairs={{0,96},{16,112},{32,64},{48,80},{64,32},{80,48},{96,0},{112,16},{1... | collective-permute-start | bytes 786440 | tf_op jit(solution)/shard_map/ppermute | solution.py:235
  84.3 1.5 %collective-permute-start.14 = (f32[8,16,512]{2,1,0:T(8,128)S(1)}, f32[8,16,512]{2,1,0:T(8,128)S(1)}, u32[]{:S(2)}, u32[]{:S(2)}) collective-permute-start(f32[8,16,512]{2,1,0:T(8,128)S(1)} %all_to_all.11.own_ref), channel_id=1, source_target_pairs={{0,1},{1,0},{2,3},{3,2},{4,5},{5,4},{6,7},{7,6},{8,9},{9,8},{10,11... | collective-permute-start | bytes 786440 | tf_op jit(solution)/shard_map/ppermute | solution.py:235
  87.7 8.8 %collective-permute-start.15 = (f32[16,2048]{1,0:T(8,128)S(1)}, f32[16,2048]{1,0:T(8,128)S(1)}, u32[]{:S(2)}, u32[]{:S(2)}) collective-permute-start(f32[16,2048]{1,0:T(8,128)S(1)} %get-tuple-element.36), channel_id=1, source_target_pairs={{0,80},{16,64},{32,112},{48,96},{64,16},{80,0},{96,48},{112,32},{1... | collective-permute-start | bytes 393224 | tf_op jit(solution)/shard_map/ppermute | solution.py:235
  88.9 14.3 %collective-permute-start.16 = (f32[16,2048]{1,0:T(8,128)S(1)}, f32[16,2048]{1,0:T(8,128)S(1)}, u32[]{:S(2)}, u32[]{:S(2)}) collective-permute-start(f32[16,2048]{1,0:T(8,128)S(1)} %get-tuple-element.37), channel_id=1, source_target_pairs={{0,64},{16,80},{32,96},{48,112},{64,0},{80,16},{96,32},{112,48},{1... | collective-permute-start | bytes 393224 | tf_op jit(solution)/shard_map/ppermute | solution.py:235
  91.5 12.0 %collective-permute-start.17 = (f32[16,2048]{1,0:T(8,128)S(1)}, f32[16,2048]{1,0:T(8,128)S(1)}, u32[]{:S(2)}, u32[]{:S(2)}) collective-permute-start(f32[16,2048]{1,0:T(8,128)S(1)} %get-tuple-element.38), channel_id=1, source_target_pairs={{0,48},{16,32},{32,16},{48,0},{64,112},{80,96},{96,80},{112,64},{1... | collective-permute-start | bytes 393224 | tf_op jit(solution)/shard_map/ppermute | solution.py:235
  92.7 10.8 %collective-permute-start.18 = (f32[16,2048]{1,0:T(8,128)S(1)}, f32[16,2048]{1,0:T(8,128)S(1)}, u32[]{:S(2)}, u32[]{:S(2)}) collective-permute-start(f32[16,2048]{1,0:T(8,128)S(1)} %get-tuple-element.39), channel_id=1, source_target_pairs={{0,112},{16,96},{32,80},{48,64},{64,48},{80,32},{96,16},{112,0},{1... | collective-permute-start | bytes 393224 | tf_op jit(solution)/shard_map/ppermute | solution.py:235
  93.9 11.1 %collective-permute-start.19 = (f32[16,2048]{1,0:T(8,128)S(1)}, f32[16,2048]{1,0:T(8,128)S(1)}, u32[]{:S(2)}, u32[]{:S(2)}) collective-permute-start(f32[16,2048]{1,0:T(8,128)S(1)} %get-tuple-element.40), channel_id=1, source_target_pairs={{0,96},{16,112},{32,64},{48,80},{64,32},{80,48},{96,0},{112,16},{1... | collective-permute-start | bytes 393224 | tf_op jit(solution)/shard_map/ppermute | solution.py:235
  96.5 8.4 %collective-permute-start.20 = (f32[16,2048]{1,0:T(8,128)S(1)}, f32[16,2048]{1,0:T(8,128)S(1)}, u32[]{:S(2)}, u32[]{:S(2)}) collective-permute-start(f32[16,2048]{1,0:T(8,128)S(1)} %get-tuple-element.41), channel_id=1, source_target_pairs={{0,32},{16,48},{32,0},{48,16},{64,96},{80,112},{96,64},{112,80},{1... | collective-permute-start | bytes 393224 | tf_op jit(solution)/shard_map/ppermute | solution.py:235
  103.3 5.0 %collective-permute-start.21 = (f32[16,2048]{1,0:T(8,128)S(1)}, f32[16,2048]{1,0:T(8,128)S(1)}, u32[]{:S(2)}, u32[]{:S(2)}) collective-permute-start(f32[16,2048]{1,0:T(8,128)S(1)} %get-tuple-element.42), channel_id=1, source_target_pairs={{0,16},{16,0},{32,48},{48,32},{64,80},{80,64},{96,112},{112,96},{1... | collective-permute-start | bytes 393224 | tf_op jit(solution)/shard_map/ppermute | solution.py:235
  (10 other events, 58.3 us)
